TPU v7x, 32 devices: a whole 2x2x4 slice. The times are simulated.
32 devices in a mesh: dp: 4 (over y, x), expert: 8 (over z, core).
Axes of the slice: x: 2, y: 2, z: 4, core: 2. Of those that a mesh axis runs over, the one named last changes fastest.
Arguments:
- tokens: bfloat16 [2, 32, 256, 1024], P(None, ('dp', 'expert')), may hold values from -6 to 6
- segment_ids: int32 [2, 32, 256], P(None, ('dp', 'expert')), may hold values from 0 to 15, never falling along the last dimension, each value on 1 to 128 neighbouring positions
- routes: int32 [2, 32, 256, 1], P(None, ('dp', 'expert')), may hold values from 0 to 7
- cotangent: bfloat16 [2, 32, 256, 1024], P(None, ('dp', 'expert')), may hold values from -6 to 6
- w_qkv: bfloat16 [1024, 3072], P(('dp', 'expert')), may hold values from -0.25 to 0.25
- w_attn_out: bfloat16 [1024, 1024], P(('dp', 'expert')), may hold values from -0.5 to 0.5
- w_router: bfloat16 [1024, 8], P(('dp', 'expert')), may hold values from -0.125 to 0.125
- gain_attn: bfloat16 [1024], P(('dp', 'expert')), may hold values from 0.099609375 to 1.8984375
- gain_moe: bfloat16 [1024], P(('dp', 'expert')), may hold values from 0.099609375 to 1.8984375
- w_expert_in: bfloat16 [8, 1024, 4096], P('expert', 'dp'), may hold values from -0.1875 to 0.1875
- w_expert_out: bfloat16 [8, 4096, 1024], P('expert', 'dp'), may hold values from -0.75 to 0.75
Outputs:
- output: bfloat16 [2, 32, 256, 1024], P(None, ('dp', 'expert'))
- grad_tokens: float32 [2, 32, 256, 1024], P(None, ('dp', 'expert'))
- grad_qkv: float32 [1024, 3072], P(('dp', 'expert'))
- grad_attn_out: float32 [1024, 1024], P(('dp', 'expert'))
- grad_router: float32 [1024, 8], P(('dp', 'expert'))
- grad_gain_attn: float32 [1024], P(('dp', 'expert'))
- grad_gain_moe: float32 [1024], P(('dp', 'expert'))
- grad_expert_in: float32 [8, 1024, 4096], P('expert', 'dp')
- grad_expert_out: float32 [8, 4096, 1024], P('expert', 'dp')
Inputs may be any that keep to these rules, and one draw needn't show every extreme that they name: `segment_ids`: in each sequence the numbers never fall; a document spans 1 to 128 positions, and in each sequence one spans exactly that many.
All inputs are finite; a program needn't handle non-finite values.
Results may differ from a plain program's by a relative error of at most 0.014.
The roundings to bfloat16 on the way count: a program that leaves them out, or rounds other values in their place, can miss the bound.
Values may be sent and summed in bfloat16 or wider, within the bound.
A program may use at most 256 MiB of HBM per device.

v0:
```python
import math
import jax
import jax.numpy as jnp
from jax import lax
from jax.sharding import PartitionSpec as P

HEADS = 16
epsilon = 1e-05
masked_value = -1e30


def normalize(values):
    row_mean = jnp.mean(values, axis=-1, keepdims=True)
    centered = values - row_mean
    inv_scale = lax.rsqrt(jnp.mean(centered * centered, axis=-1, keepdims=True) + epsilon)
    return (centered * inv_scale, inv_scale)


def norm_back(grad_normed, normed, inv_scale):
    return inv_scale * (
        grad_normed
        - jnp.mean(grad_normed, axis=-1, keepdims=True)
        - normed * jnp.mean(grad_normed * normed, axis=-1, keepdims=True)
    )


def fetch_attention(attn_local):
    return (
        lax.all_gather(attn_local[0], ("dp", "expert"), axis=0, tiled=True),
        lax.all_gather(attn_local[1], ("dp", "expert"), axis=0, tiled=True),
        lax.all_gather(attn_local[2], ("dp", "expert"), axis=0, tiled=True),
        lax.all_gather(attn_local[3], ("dp", "expert"), axis=0, tiled=True),
        lax.all_gather(attn_local[4], ("dp", "expert"), axis=0, tiled=True),
    )


def fetch_experts(expert_local):
    return (
        lax.all_gather(expert_local[0], "dp", axis=1, tiled=True),
        lax.all_gather(expert_local[1], "dp", axis=1, tiled=True),
    )


def score_block(query_rows, key_rows, allowed, score_scale):
    scores = (
        jnp.einsum("shd,thd->hst", query_rows, key_rows, preferred_element_type=jnp.float32)
        * score_scale
    )
    return jnp.where(allowed[None], scores, masked_value)


def split_heads(qkv_rows, model_width):
    seq_len = qkv_rows.shape[0]
    head_dim = model_width // HEADS
    query_rows = qkv_rows[:, :model_width].reshape(seq_len, HEADS, head_dim)
    key_rows = qkv_rows[:, model_width : 2 * model_width].reshape(seq_len, HEADS, head_dim)
    value_rows = qkv_rows[:, 2 * model_width :].reshape(seq_len, HEADS, head_dim)
    return (query_rows, key_rows, value_rows)


def route_selector(route_row, expert_count, capacity):
    one_hot = (route_row[:, None] == lax.iota(jnp.int32, expert_count)[None, :]).astype(jnp.int32)
    earlier = jnp.cumsum(one_hot, axis=0, dtype=jnp.int32) - one_hot
    position = jnp.sum(earlier * one_hot, axis=1, dtype=jnp.int32)
    slot_index = jnp.where(position < capacity, route_row * capacity + position, -1)
    columns = lax.iota(jnp.int32, expert_count * capacity)
    selector = (slot_index[:, None] == columns[None, :]).astype(jnp.bfloat16)
    return (one_hot.astype(jnp.float32), selector)


def layer_forward(inputs, segment_row, route_row, attn_full, expert_full, capacity):
    w_qkv, w_attn_out, w_router, gain_attn, gain_moe = attn_full
    seq_len, model_width = inputs.shape
    expert_count = w_router.shape[1]
    score_scale = 1.0 / math.sqrt(model_width // HEADS)
    normed_one, inv_one = normalize(inputs)
    attn_in = (normed_one * gain_attn.astype(jnp.float32)).astype(jnp.bfloat16)
    qkv_rows = jnp.dot(attn_in, w_qkv, preferred_element_type=jnp.float32).astype(jnp.bfloat16)
    query_rows, key_rows, value_rows = split_heads(qkv_rows, model_width)
    position = lax.iota(jnp.int32, seq_len)
    allowed = (position[None, :] <= position[:, None]) & (
        segment_row[:, None] == segment_row[None, :]
    )
    masked = score_block(query_rows, key_rows, allowed, score_scale)
    row_max = jnp.max(masked, axis=-1, keepdims=True)
    log_norm = row_max + jnp.log(jnp.sum(jnp.exp(masked - row_max), axis=-1, keepdims=True))
    attn_prob = jnp.exp(masked - log_norm).astype(jnp.bfloat16)
    attn_mixed = jnp.einsum(
        "hst,thd->shd", attn_prob, value_rows, preferred_element_type=jnp.float32
    )
    attn_mixed = attn_mixed.reshape(seq_len, model_width).astype(jnp.bfloat16)
    residual = inputs + jnp.dot(attn_mixed, w_attn_out, preferred_element_type=jnp.float32)
    normed_two, inv_two = normalize(residual)
    hidden_in = (normed_two * gain_moe.astype(jnp.float32)).astype(jnp.bfloat16)
    router_prob = jax.nn.softmax(
        jnp.dot(hidden_in, w_router, preferred_element_type=jnp.float32), axis=-1
    )
    one_hot, selector = route_selector(route_row, expert_count, capacity)
    gate_prob = jnp.sum(router_prob * one_hot, axis=1)
    buffer = jnp.einsum("sc,sd->cd", selector, hidden_in, preferred_element_type=jnp.float32)
    buffer = buffer.astype(jnp.bfloat16).reshape(expert_count, capacity, model_width)
    received = lax.all_to_all(buffer, "expert", split_axis=0, concat_axis=0, tiled=True).reshape(
        expert_count * capacity, model_width
    )
    pre_act = jnp.dot(received, expert_full[0][0], preferred_element_type=jnp.float32)
    activation = jax.nn.gelu(pre_act).astype(jnp.bfloat16)
    expert_rows = jnp.dot(activation, expert_full[1][0], preferred_element_type=jnp.float32)
    expert_rows = expert_rows.astype(jnp.bfloat16).reshape(expert_count, capacity, model_width)
    returned = lax.all_to_all(
        expert_rows, "expert", split_axis=0, concat_axis=0, tiled=True
    ).reshape(expert_count * capacity, model_width)
    moe_rows = jnp.einsum("sc,cd->sd", selector, returned, preferred_element_type=jnp.float32)
    output = residual + gate_prob[:, None] * moe_rows
    forward_state = (
        normed_one,
        inv_one,
        attn_in,
        qkv_rows,
        allowed,
        log_norm,
        attn_mixed,
        normed_two,
        inv_two,
        hidden_in,
        router_prob,
        one_hot,
        selector,
        gate_prob,
        received,
        pre_act,
        activation,
        moe_rows,
    )
    return (output, forward_state)


def layer_backward(grad_out, attn_full, expert_full, forward_state):
    (
        normed_one,
        inv_one,
        attn_in,
        qkv_rows,
        allowed,
        log_norm,
        attn_mixed,
        normed_two,
        inv_two,
        hidden_in,
        router_prob,
        one_hot,
        selector,
        gate_prob,
        received,
        pre_act,
        activation,
        moe_rows,
    ) = forward_state
    w_qkv, w_attn_out, w_router, gain_attn, gain_moe = attn_full
    w_in = expert_full[0][0]
    w_out = expert_full[1][0]
    seq_len, model_width = grad_out.shape
    expert_count = w_router.shape[1]
    capacity = selector.shape[1] // expert_count
    score_scale = 1.0 / math.sqrt(model_width // HEADS)
    grad_gate = jnp.sum(grad_out * moe_rows, axis=1)
    grad_moe = (gate_prob[:, None] * grad_out).astype(jnp.bfloat16)
    grad_buffer = jnp.einsum("sc,sd->cd", selector, grad_moe, preferred_element_type=jnp.float32)
    grad_buffer = grad_buffer.astype(jnp.bfloat16).reshape(expert_count, capacity, model_width)
    grad_rows = lax.all_to_all(
        grad_buffer, "expert", split_axis=0, concat_axis=0, tiled=True
    ).reshape(expert_count * capacity, model_width)
    grad_activation = jnp.einsum("rd,fd->rf", grad_rows, w_out, preferred_element_type=jnp.float32)
    term_out = jnp.einsum("rf,rd->fd", activation, grad_rows, preferred_element_type=jnp.float32)
    gelu_slope = jax.vjp(jax.nn.gelu, pre_act)[1]
    grad_pre = gelu_slope(grad_activation)[0].astype(jnp.bfloat16)
    term_in = jnp.einsum("rd,rf->df", received, grad_pre, preferred_element_type=jnp.float32)
    grad_received = jnp.einsum("rf,df->rd", grad_pre, w_in, preferred_element_type=jnp.float32)
    grad_received = grad_received.astype(jnp.bfloat16).reshape(expert_count, capacity, model_width)
    grad_back = lax.all_to_all(
        grad_received, "expert", split_axis=0, concat_axis=0, tiled=True
    ).reshape(expert_count * capacity, model_width)
    grad_hidden = jnp.einsum("sc,cd->sd", selector, grad_back, preferred_element_type=jnp.float32)
    grad_choice = one_hot * grad_gate[:, None]
    grad_logit = router_prob * (
        grad_choice - jnp.sum(router_prob * grad_choice, axis=1, keepdims=True)
    )
    grad_logit = grad_logit.astype(jnp.bfloat16)
    term_router = jnp.einsum("sd,se->de", hidden_in, grad_logit, preferred_element_type=jnp.float32)
    grad_hidden = grad_hidden + jnp.einsum(
        "se,de->sd", grad_logit, w_router, preferred_element_type=jnp.float32
    )
    term_gain_moe = jnp.sum(grad_hidden * normed_two, axis=0)
    grad_resid = grad_out + norm_back(
        grad_hidden * gain_moe.astype(jnp.float32), normed_two, inv_two
    )
    grad_branch = grad_resid.astype(jnp.bfloat16)
    term_attn_out = jnp.einsum(
        "sd,se->de", attn_mixed, grad_branch, preferred_element_type=jnp.float32
    )
    grad_mixed = jnp.einsum(
        "se,de->sd", grad_branch, w_attn_out, preferred_element_type=jnp.float32
    )
    grad_mixed = grad_mixed.astype(jnp.bfloat16).reshape(seq_len, HEADS, model_width // HEADS)
    query_rows, key_rows, value_rows = split_heads(qkv_rows, model_width)
    masked = score_block(query_rows, key_rows, allowed, score_scale)
    attn_prob = jnp.exp(masked - log_norm)
    grad_prob = jnp.einsum(
        "shd,thd->hst", grad_mixed, value_rows, preferred_element_type=jnp.float32
    )
    grad_value = jnp.einsum(
        "hst,shd->thd",
        attn_prob.astype(jnp.bfloat16),
        grad_mixed,
        preferred_element_type=jnp.float32,
    )
    grad_score = attn_prob * (grad_prob - jnp.sum(attn_prob * grad_prob, axis=-1, keepdims=True))
    grad_score = grad_score.astype(jnp.bfloat16)
    grad_query = (
        jnp.einsum("hst,thd->shd", grad_score, key_rows, preferred_element_type=jnp.float32)
        * score_scale
    )
    grad_key = (
        jnp.einsum("hst,shd->thd", grad_score, query_rows, preferred_element_type=jnp.float32)
        * score_scale
    )
    grad_qkv_rows = jnp.concatenate(
        [
            grad_query.reshape(seq_len, model_width),
            grad_key.reshape(seq_len, model_width),
            grad_value.reshape(seq_len, model_width),
        ],
        axis=1,
    ).astype(jnp.bfloat16)
    term_qkv = jnp.einsum("sd,sf->df", attn_in, grad_qkv_rows, preferred_element_type=jnp.float32)
    grad_attn_in = jnp.einsum("sf,df->sd", grad_qkv_rows, w_qkv, preferred_element_type=jnp.float32)
    term_gain_attn = jnp.sum(grad_attn_in * normed_one, axis=0)
    grad_inputs = grad_resid + norm_back(
        grad_attn_in * gain_attn.astype(jnp.float32), normed_one, inv_one
    )
    attn_terms = (term_qkv, term_attn_out, term_router, term_gain_attn, term_gain_moe)
    expert_terms = (term_in[None], term_out[None])
    return (grad_inputs, attn_terms, expert_terms)


def on_device(
    tokens,
    segment_ids,
    routes,
    cotangent,
    w_qkv,
    w_attn_out,
    w_router,
    gain_attn,
    gain_moe,
    w_expert_in,
    w_expert_out,
):
    micro_count = tokens.shape[0]
    seq_len = tokens.shape[2]
    expert_count = w_router.shape[1]
    capacity = (9 * seq_len + 8 * expert_count - 1) // (8 * expert_count)
    attn_local = (w_qkv, w_attn_out, w_router, gain_attn, gain_moe)
    expert_local = (w_expert_in, w_expert_out)
    attn_total = None
    expert_total = None
    outputs = []
    grads_in = []
    for micro_idx in range(micro_count):
        attn_full = fetch_attention(attn_local)
        expert_full = fetch_experts(expert_local)
        inputs = tokens[micro_idx, 0].astype(jnp.float32)
        output, forward_state = layer_forward(
            inputs,
            segment_ids[micro_idx, 0],
            routes[micro_idx, 0, :, 0],
            attn_full,
            expert_full,
            capacity,
        )
        outputs.append(output.astype(jnp.bfloat16))
        attn_full = fetch_attention(attn_local)
        expert_full = fetch_experts(expert_local)
        grad_inputs, attn_terms, expert_terms = layer_backward(
            cotangent[micro_idx, 0].astype(jnp.float32), attn_full, expert_full, forward_state
        )
        grads_in.append(grad_inputs)
        attn_total = (
            attn_terms if attn_total is None else jax.tree.map(jnp.add, attn_total, attn_terms)
        )
        expert_total = (
            expert_terms
            if expert_total is None
            else jax.tree.map(jnp.add, expert_total, expert_terms)
        )
    attn_total = (
        lax.psum_scatter(attn_total[0], ("dp", "expert"), scatter_dimension=0, tiled=True),
        lax.psum_scatter(attn_total[1], ("dp", "expert"), scatter_dimension=0, tiled=True),
        lax.psum_scatter(attn_total[2], ("dp", "expert"), scatter_dimension=0, tiled=True),
        lax.psum_scatter(attn_total[3], ("dp", "expert"), scatter_dimension=0, tiled=True),
        lax.psum_scatter(attn_total[4], ("dp", "expert"), scatter_dimension=0, tiled=True),
    )
    expert_total = (
        lax.psum_scatter(
            expert_total[0].astype(jnp.bfloat16), "dp", scatter_dimension=1, tiled=True
        ).astype(jnp.float32),
        lax.psum_scatter(
            expert_total[1].astype(jnp.bfloat16), "dp", scatter_dimension=1, tiled=True
        ).astype(jnp.float32),
    )
    output_all = jnp.stack(outputs)[:, None]
    grad_tokens = jnp.stack(grads_in)[:, None]
    return (
        output_all,
        grad_tokens,
        attn_total[0],
        attn_total[1],
        attn_total[2],
        attn_total[3],
        attn_total[4],
        expert_total[0],
        expert_total[1],
    )


def solution(mesh):
    in_specs = (
        P(None, ("dp", "expert"), None, None),
        P(None, ("dp", "expert"), None),
        P(None, ("dp", "expert"), None, None),
        P(None, ("dp", "expert"), None, None),
        P(("dp", "expert"), None),
        P(("dp", "expert"), None),
        P(("dp", "expert"), None),
        P(("dp", "expert")),
        P(("dp", "expert")),
        P("expert", "dp", None),
        P("expert", "dp", None),
    )
    out_specs = (
        P(None, ("dp", "expert"), None, None),
        P(None, ("dp", "expert"), None, None),
        P(("dp", "expert"), None),
        P(("dp", "expert"), None),
        P(("dp", "expert"), None),
        P(("dp", "expert")),
        P(("dp", "expert")),
        P("expert", "dp", None),
        P("expert", "dp", None),
    )
    return jax.shard_map(
        on_device, mesh=mesh, in_specs=in_specs, out_specs=out_specs, check_vma=False
    )
```

profile of v0, /device:TPU:0, one launch (start us, length us, event | category | flops | bytes accessed | tf_op | source)
XLA Modules:
  0.0 1070.3 jit_solution(837478429790069913)
XLA Ops:
  10.5 42.6 %all-reduce.5 = (bf16[1024]{0:T(1024)(128)(2,1)S(1)}, bf16[1024]{0:T(1024)(128)(2,1)S(1)}) all-reduce(bf16[1024]{0:T(1024)(128)(2,1)S(1)} %dynamic-update-slice, bf16[1024]{0:T(1024)(128)(2,1)S(1)} %dynamic-update-slice.1), channel_id=1, replica_groups=mesh['dp'=4,'expert'=8] {'dp','expert'}, use_global_device_ids=true, to_apply=%add | all-reduce | flops 2048 | bytes 8192
  55.1 28.3 %all-gather.6.cloned.1.call-done = bf16[1024,3072]{1,0:T(8,128)(2,1)} async-done(((bf16[32,3072]{1,0:T(8,128)(2,1)}), bf16[1024,3072]{1,0:T(8,128)(2,1)}) %all-gather.6.cloned.1.call-update) | async-done | bytes 6291472 | tf_op jit(solution)/shard_map/all_gather | solution.py:29
  102.8 38.5 %all-gather.8.cloned.1.call-done = bf16[1024,1024]{1,0:T(8,128)(2,1)} async-done(((bf16[32,1024]{1,0:T(8,128)(2,1)}), bf16[1024,1024]{1,0:T(8,128)(2,1)}) %all-gather.8.cloned.1.call-update) | async-done | bytes 2097168 | tf_op jit(solution)/shard_map/all_gather | solution.py:30
  159.8 13.8 %all-to-all-done.2 = bf16[8,36,1024]{2,1,0:T(8,128)(2,1)S(1)} async-done(((bf16[8,36,1024]{2,1,0:T(8,128)(2,1)}), bf16[8,36,1024]{2,1,0:T(8,128)(2,1)S(1)}, u32[]{:S(2)}, u32[]{:S(2)}) %all-to-all-start.2) | async-done | bytes 589856 | tf_op jit(solution)/shard_map/all_to_all | solution.py:102
  178.8 50.8 %all-gather.10.cloned.1.call-done = bf16[1,1024,4096]{2,1,0:T(8,128)(2,1)} async-done(((bf16[1,256,4096]{2,1,0:T(8,128)(2,1)}), bf16[1,1024,4096]{2,1,0:T(8,128)(2,1)}) %all-gather.10.cloned.1.call-update) | async-done | bytes 8388624 | tf_op jit(solution)/shard_map/all_gather | solution.py:39
  229.5 8.3 fusion.14
  237.8 80.9 %all-gather.12.cloned.1.call-done = bf16[1,4096,1024]{2,1,0:T(8,128)(2,1)} async-done(((bf16[1,1024,1024]{2,1,0:T(8,128)(2,1)}), bf16[1,4096,1024]{2,1,0:T(8,128)(2,1)}) %all-gather.12.cloned.1.call-update) | async-done | bytes 8388624 | tf_op jit(solution)/shard_map/all_gather | solution.py:40
  318.8 7.8 fusion.49
  340.8 7.3 fusion.46
  355.2 47.5 %all-gather = bf16[32,32,8]{1,2,0:T(8,128)(2,1)S(1)} all-gather(bf16[1,32,8]{1,2,0:T(8,128)(2,1)S(1)} %bitcast.292), channel_id=1, replica_groups=mesh['dp'=4,'expert'=8] {'dp','expert'}, dimensions={0}, use_global_device_ids=true | all-gather | bytes 16896 | tf_op jit(solution)/shard_map/all_gather | solution.py:31
  424.6 14.2 %all-to-all-done.4 = bf16[8,36,1024]{2,1,0:T(8,128)(2,1)} async-done(((bf16[8,36,1024]{2,1,0:T(8,128)(2,1)}), bf16[8,36,1024]{2,1,0:T(8,128)(2,1)}, u32[]{:S(2)}, u32[]{:S(2)}) %all-to-all-start.4) | async-done | bytes 589856 | tf_op jit(solution)/shard_map/all_to_all | solution.py:169
  446.9 13.2 %fusion.177 = f32[4096,1024]{1,0:T(8,128)} fusion(bf16[288,1024]{1,0:T(8,128)(2,1)} %reshape.406, f32[288,4096]{1,0:T(8,128)} %copy-done.15), kind=kOutput, calls=%fused_computation.253 | convolution fusion | flops 2426535936 | bytes 22085632 | tf_op jit(solution)/shard_map/rf,rd->fd/dot_general | solution.py:173
  461.7 15.6 %fusion.1 = bf16[1,4096,1024]{2,1,0:T(8,128)(2,1)} fusion(f32[4096,1024]{1,0:T(8,128)} %fusion.177, bf16[288,1024]{1,0:T(8,128)(2,1)} %reshape.414, f32[288,4096]{1,0:T(8,128)} %fusion.14), kind=kOutput, calls=%fused_computation.3 | convolution fusion | flops 2434924544 | bytes 30474240 | tf_op jit(solution)/shard_map/rf,rd->fd/dot_general | solution.py:173
  478.3 11.6 %fusion.24 = bf16[288,4096]{1,0:T(8,128)(2,1)S(1)} fusion(f32[288,4096]{1,0:T(8,128)} %copy-done.15, bf16[288,1024]{1,0:T(8,128)(2,1)S(1)} %copy-done.28, bf16[1,4096,1024]{2,1,0:T(8,128)(2,1)} %all-gather.12.cloned.1.call-done), kind=kOutput, calls=%fused_computation.31 | convolution fusion | flops 2439512064 | bytes 16056320 | tf_op jit(solution)/shard_map/rd,fd->rf/dot_general | solution.py:172
  490.0 8.1 fusion.186
  498.1 11.7 %fusion.31 = bf16[288,4096]{1,0:T(8,128)(2,1)S(1)} fusion(f32[288,4096]{1,0:T(8,128)} %fusion.14, bf16[288,1024]{1,0:T(8,128)(2,1)S(1)} %copy-done.30, bf16[1,4096,1024]{2,1,0:T(8,128)(2,1)} %all-gather.12.cloned.1.call-done), kind=kOutput, calls=%fused_computation.38 | convolution fusion | flops 2439512064 | bytes 16056320 | tf_op jit(solution)/shard_map/rd,fd->rf/dot_general | solution.py:172
  511.2 10.3 fusion
  541.3 11.1 %all-to-all-done.5 = bf16[8,36,1024]{2,1,0:T(8,128)(2,1)S(1)} async-done(((bf16[8,36,1024]{2,1,0:T(8,128)(2,1)}), bf16[8,36,1024]{2,1,0:T(8,128)(2,1)S(1)}, u32[]{:S(2)}, u32[]{:S(2)}) %all-to-all-start.5) | async-done | bytes 589856 | tf_op jit(solution)/shard_map/all_to_all | solution.py:179
  556.9 17.4 %all-to-all-done.7 = bf16[8,36,1024]{2,1,0:T(8,128)(2,1)S(1)} async-done(((bf16[8,36,1024]{2,1,0:T(8,128)(2,1)}), bf16[8,36,1024]{2,1,0:T(8,128)(2,1)S(1)}, u32[]{:S(2)}, u32[]{:S(2)}) %all-to-all-start.7) | async-done | bytes 589856 | tf_op jit(solution)/shard_map/all_to_all | solution.py:179
  624.0 6.8 fusion.84
  630.9 37.4 %all-reduce.4 = (f32[1024]{0:T(1024)S(1)}, f32[1024]{0:T(1024)S(1)}) all-reduce(f32[1024]{0:T(1024)S(1)} %add.172, f32[1024]{0:T(1024)S(1)} %add.173), channel_id=5, replica_groups=mesh['dp'=4,'expert'=8] {'dp','expert'}, use_global_device_ids=true, to_apply=%region_43.44.clone | all-reduce | flops 2048 | bytes 16384
  679.7 78.5 %reduce-scatter.12.cloned.1.call-done = bf16[1,256,4096]{2,1,0:T(8,128)(2,1)} async-done(((bf16[1,1024,4096]{2,1,0:T(8,128)(2,1)}), bf16[1,256,4096]{2,1,0:T(8,128)(2,1)}) %reduce-scatter.12.cloned.1.call-update) | async-done | bytes 2097168 | tf_op jit(solution)/shard_map/reduce_scatter | solution.py:303
  762.2 142.7 %reduce-scatter.10.cloned.1.call-done = f32[32,1024]{1,0:T(8,128)} async-done(((f32[1024,1024]{1,0:T(8,128)}), f32[32,1024]{1,0:T(8,128)}) %reduce-scatter.10.cloned.1.call-update) | async-done | bytes 131088 | tf_op jit(solution)/shard_map/reduce_scatter | solution.py:297
  904.9 158.4 %reduce-scatter.8.cloned.1.call-done = f32[32,3072]{1,0:T(8,128)} async-done(((f32[1024,3072]{1,0:T(8,128)}), f32[32,3072]{1,0:T(8,128)}) %reduce-scatter.8.cloned.1.call-update) | async-done | bytes 393232 | tf_op jit(solution)/shard_map/reduce_scatter | solution.py:296
  (308 shorter events, 191.7 us)
Async XLA Ops:
  7.2 45.9 %copy-start.66 = (s32[2,1,256,1]{2,3,1,0:T(1,128)S(1)}, s32[2,1,256,1]{2,3,1,0:T(1,128)}, u32[]{:S(2)}) copy-start(s32[2,1,256,1]{2,3,1,0:T(1,128)} %param.13) | copy-start | bytes 6148
  7.2 46.9 %copy-start.6 = (bf16[2,1,256,1024]{3,2,1,0:T(8,128)(2,1)S(1)}, bf16[2,1,256,1024]{3,2,1,0:T(8,128)(2,1)}, u32[]{:S(2)}) copy-start(bf16[2,1,256,1024]{3,2,1,0:T(8,128)(2,1)} %param.11) | copy-start | bytes 3145732
  7.2 47.6 %copy-start.67 = (s32[2,1,256]{2,1,0:T(1,128)S(1)}, s32[2,1,256]{2,1,0:T(1,128)}, u32[]{:S(2)}) copy-start(s32[2,1,256]{2,1,0:T(1,128)} %param.12) | copy-start | bytes 6148
  7.2 76.2 %all-gather.6.cloned.1.call-start = ((), (), s32[]{:S(2)}) async-start(), calls=%async_computation.13 | async-start | bytes 6488064 | tf_op jit(solution)/shard_map/all_gather | solution.py:29
  8.0 133.4 %all-gather.8.cloned.1.call-start = ((), (), s32[]{:S(2)}) async-start(), calls=%async_computation.14 | async-start | bytes 2162688 | tf_op jit(solution)/shard_map/all_gather | solution.py:30
  8.7 220.8 %all-gather.10.cloned.1.call-start = ((), (), s32[]{:S(2)}) async-start(), calls=%async_computation.15 | async-start | bytes 10485760 | tf_op jit(solution)/shard_map/all_gather | solution.py:39
  9.4 309.3 %all-gather.12.cloned.1.call-start = ((), (), s32[]{:S(2)}) async-start(), calls=%async_computation.16 | async-start | bytes 10485760 | tf_op jit(solution)/shard_map/all_gather | solution.py:40
  54.9 91.0 %copy-start.42 = (pred[256,256]{0,1:T(8,128)(4,1)}, pred[256,256]{0,1:T(8,128)(4,1)S(1)}, u32[]{:S(2)}) copy-start(pred[256,256]{0,1:T(8,128)(4,1)S(1)} %fusion.112) | copy-start | bytes 196612
  88.5 55.7 %copy-start.16 = (bf16[256,1024]{0,1:T(8,128)(2,1)}, bf16[256,1024]{0,1:T(8,128)(2,1)S(1)}, u32[]{:S(2)}) copy-start(bf16[256,1024]{0,1:T(8,128)(2,1)S(1)} %copy.72) | copy-start | bytes 1572868
  149.9 253.0 %copy-start.14 = (bf16[256,1024]{1,0:T(8,128)(2,1)}, bf16[256,1024]{1,0:T(8,128)(2,1)S(1)}, u32[]{:S(2)}) copy-start(bf16[256,1024]{1,0:T(8,128)(2,1)S(1)} %get-tuple-element.79) | copy-start | bytes 1572868
  152.0 21.6 %all-to-all-start.2 = ((bf16[8,36,1024]{2,1,0:T(8,128)(2,1)}), bf16[8,36,1024]{2,1,0:T(8,128)(2,1)S(1)}, u32[]{:S(2)}, u32[]{:S(2)}) async-start(bf16[8,36,1024]{2,1,0:T(8,128)(2,1)} %reshape.401), calls=%async_computation.2 | async-start | bytes 1310720 | tf_op jit(solution)/shard_map/all_to_all | solution.py:102
  173.7 153.9 %all-to-all-start = ((bf16[8,36,1024]{2,1,0:T(8,128)(2,1)}), bf16[8,36,1024]{2,1,0:T(8,128)(2,1)}, u32[]{:S(2)}, u32[]{:S(2)}) async-start(bf16[8,36,1024]{2,1,0:T(8,128)(2,1)} %reshape.393), calls=%async_computation | async-start | bytes 1310720 | tf_op jit(solution)/shard_map/all_to_all | solution.py:102
  327.6 22.9 %all-to-all-start.3 = ((bf16[8,36,1024]{2,1,0:T(8,128)(2,1)}), bf16[8,36,1024]{2,1,0:T(8,128)(2,1)}, u32[]{:S(2)}, u32[]{:S(2)}) async-start(bf16[8,36,1024]{2,1,0:T(8,128)(2,1)} %reshape.403), calls=%async_computation.3 | async-start | bytes 1310720 | tf_op jit(solution)/shard_map/all_to_all | solution.py:109
  350.4 56.3 %all-to-all-start.1 = ((bf16[8,36,1024]{2,1,0:T(8,128)(2,1)}), bf16[8,36,1024]{2,1,0:T(8,128)(2,1)}, u32[]{:S(2)}, u32[]{:S(2)}) async-start(bf16[8,36,1024]{2,1,0:T(8,128)(2,1)} %reshape.395), calls=%async_computation.1 | async-start | bytes 1310720 | tf_op jit(solution)/shard_map/all_to_all | solution.py:109
  416.5 22.3 %all-to-all-start.4 = ((bf16[8,36,1024]{2,1,0:T(8,128)(2,1)}), bf16[8,36,1024]{2,1,0:T(8,128)(2,1)}, u32[]{:S(2)}, u32[]{:S(2)}) async-start(bf16[8,36,1024]{2,1,0:T(8,128)(2,1)} %reshape.405), calls=%async_computation.4 | async-start | bytes 1310720 | tf_op jit(solution)/shard_map/all_to_all | solution.py:169
  438.8 22.0 %all-to-all-start.6 = ((bf16[8,36,1024]{2,1,0:T(8,128)(2,1)}), bf16[8,36,1024]{2,1,0:T(8,128)(2,1)S(1)}, u32[]{:S(2)}, u32[]{:S(2)}) async-start(bf16[8,36,1024]{2,1,0:T(8,128)(2,1)} %reshape.413), calls=%async_computation.6 | async-start | bytes 1310720 | tf_op jit(solution)/shard_map/all_to_all | solution.py:169
  442.3 175.1 %reduce-scatter.16.cloned.1.call-start = ((), (), s32[]{:S(2)}) async-start(), calls=%async_computation.21 | async-start | bytes 540672
  444.9 230.7 %reduce-scatter.14.cloned.1.call-start = ((), (), s32[]{:S(2)}) async-start(), calls=%async_computation.20 | async-start | bytes 10485760 | tf_op jit(solution)/shard_map/reduce_scatter | solution.py:306
  477.3 280.8 %reduce-scatter.12.cloned.1.call-start = ((), (), s32[]{:S(2)}) async-start(), calls=%async_computation.19 | async-start | bytes 10485760 | tf_op jit(solution)/shard_map/reduce_scatter | solution.py:303
  529.2 23.1 %all-to-all-start.5 = ((bf16[8,36,1024]{2,1,0:T(8,128)(2,1)}), bf16[8,36,1024]{2,1,0:T(8,128)(2,1)S(1)}, u32[]{:S(2)}, u32[]{:S(2)}) async-start(bf16[8,36,1024]{2,1,0:T(8,128)(2,1)} %reshape.407), calls=%async_computation.5 | async-start | bytes 1310720 | tf_op jit(solution)/shard_map/all_to_all | solution.py:179
  552.4 22.0 %all-to-all-start.7 = ((bf16[8,36,1024]{2,1,0:T(8,128)(2,1)}), bf16[8,36,1024]{2,1,0:T(8,128)(2,1)S(1)}, u32[]{:S(2)}, u32[]{:S(2)}) async-start(bf16[8,36,1024]{2,1,0:T(8,128)(2,1)} %reshape.415), calls=%async_computation.7 | async-start | bytes 1310720 | tf_op jit(solution)/shard_map/all_to_all | solution.py:179
  555.9 349.0 %reduce-scatter.10.cloned.1.call-start = ((), (), s32[]{:S(2)}) async-start(), calls=%async_computation.18 | async-start | bytes 4325376 | tf_op jit(solution)/shard_map/reduce_scatter | solution.py:297
  584.2 479.0 %reduce-scatter.8.cloned.1.call-start = ((), (), s32[]{:S(2)}) async-start(), calls=%async_computation.17 | async-start | bytes 12976128 | tf_op jit(solution)/shard_map/reduce_scatter | solution.py:296
  624.0 47.7 %copy-start.9 = (f32[256,1024]{1,0:T(8,128)S(1)}, f32[256,1024]{1,0:T(8,128)}, u32[]{:S(2)}) copy-start(f32[256,1024]{1,0:T(8,128)} %copy-done.8) | copy-start | bytes 3145732
  (64 other events, 497.9 us)
Sparse Core Ops, SparseCore 0:
  11.0 72.3 all-gather.5
  86.4 54.8 all-gather.7
  143.2 86.3 all-gather.9
  231.2 87.4 all-gather.11
  445.1 136.7 reduce-scatter.15
  584.8 83.8 reduce-scatter.13
  671.8 86.3 reduce-scatter.11
  761.0 143.8 reduce-scatter.9
  911.5 151.7 reduce-scatter.7
where the time goes:
time: 1080 us; the launch traced here: 1070 us
  waiting for transfers between devices  638 us (59%)
  matrix products  186 us (17%)
  blocking collectives  128 us (12%)
  local copies, waits for them, and re-layouts  45.5 us (4%)
  starting transfers between devices  33.8 us (3%)
  other arithmetic  23.6 us (2%)
  between operations  15.6 us (1%)
    reduce_scatter x1, waiting for transfers between devices, on_device(): lax.psum_scatter(attn_total[0], ('dp', 'expert'), scatter_dimension=0, ti...  158 us
    reduce_scatter x1, waiting for transfers between devices, on_device(): lax.psum_scatter(attn_total[1], ('dp', 'expert'), scatter_dimension=0, ti...  143 us
    all_gather x1, waiting for transfers between devices, fetch_experts(): lax.all_gather(expert_local[1], 'dp', axis=1, tiled=True)  80.9 us
    unnamed x2, blocking collectives  80 us
    reduce_scatter x1, waiting for transfers between devices, on_device(): lax.psum_scatter(expert_total[0].astype(jnp.bfloat16), 'dp', scatter_dime...  78.5 us
    all_gather x1, waiting for transfers between devices, fetch_experts(): lax.all_gather(expert_local[0], 'dp', axis=1, tiled=True)  50.8 us
    all_gather x1, blocking collectives, fetch_attention(): lax.all_gather(attn_local[2], ('dp', 'expert'), axis=0, tiled=True)  47.5 us
    all_gather x1, waiting for transfers between devices, fetch_attention(): lax.all_gather(attn_local[1], ('dp', 'expert'), axis=0, tiled=True)  38.5 us
  transfers between devices with their start and end apart: 17, of which 13 were waited for; matrix products, arithmetic and copies ran while one was open for 22% of the time, Pallas kernels for 0%

commit v1 on v0

--- a/solution.py
+++ b/solution.py
@@ -1,3 +1,4 @@
+import functools
 import math
 import jax
 import jax.numpy as jnp
@@ -9,6 +10,17 @@
 masked_value = -1e30
 
 
+def drive_pairs_all(packet, bus_axis, array_axis):
+    carry_out = lax.axis_size(bus_axis)
+    all_rows = jnp.stack(carry_out * [packet], axis=0)
+    big = lax.all_to_all(all_rows, bus_axis, 0, 0)
+    long_array = jnp.concatenate(big, axis=array_axis)
+    return long_array
+
+
+outputs_lift = functools.partial(drive_pairs_all, bus_axis=("dp", "expert"), array_axis=0)
+
+
 def normalize(values):
     row_mean = jnp.mean(values, axis=-1, keepdims=True)
     centered = values - row_mean
@@ -27,7 +39,7 @@
 def fetch_attention(attn_local):
     return (
         lax.all_gather(attn_local[0], ("dp", "expert"), axis=0, tiled=True),
-        lax.all_gather(attn_local[1], ("dp", "expert"), axis=0, tiled=True),
+        outputs_lift(attn_local[1]),
         lax.all_gather(attn_local[2], ("dp", "expert"), axis=0, tiled=True),
         lax.all_gather(attn_local[3], ("dp", "expert"), axis=0, tiled=True),
         lax.all_gather(attn_local[4], ("dp", "expert"), axis=0, tiled=True),

time: 1080 us -> 1030 us (0.954)
  waiting for transfers between devices: 638 us -> 549 us
  blocking collectives: 128 us -> 173 us
    unnamed x2, blocking collectives: 80 us -> 125 us
    all_gather x1 -> x0, waiting for transfers between devices: 38.5 us -> none  [fetch_attention(): lax.all_gather(attn_local[1], ('dp', 'expert'), axis=0, tiled=True)]
    all_gather x1, waiting for transfers between devices: 50.8 us -> 13.9 us  [fetch_experts(): lax.all_gather(expert_local[0], 'dp', axis=1, tiled=True)]
    all_gather x1, waiting for transfers between devices: 28.3 us -> 0.02 us  [fetch_attention(): lax.all_gather(attn_local[0], ('dp', 'expert'), axis=0, tiled=True)]
  transfers between devices with their start and end apart: 17 -> 17, of which waited for: 13 -> 11; matrix products, arithmetic and copies ran while one was open for 22% -> 23% of each run, Pallas kernels for 0% -> 0%
where the time goes in v1:
time: 1030 us; the launch traced here: 1020 us
  waiting for transfers between devices  549 us (53%)
  matrix products  176 us (17%)
  blocking collectives  173 us (17%)
  local copies, waits for them, and re-layouts  46.6 us (5%)
  starting transfers between devices  38.2 us (4%)
  other arithmetic  24.1 us (2%)
  between operations  15.7 us (2%)
    reduce_scatter x1, waiting for transfers between devices, on_device(): lax.psum_scatter(attn_total[0], ('dp', 'expert'), scatter_dimension=0, ti...  159 us
    reduce_scatter x1, waiting for transfers between devices, on_device(): lax.psum_scatter(attn_total[1], ('dp', 'expert'), scatter_dimension=0, ti...  143 us
    unnamed x2, blocking collectives  125 us
    all_gather x1, waiting for transfers between devices, fetch_experts(): lax.all_gather(expert_local[1], 'dp', axis=1, tiled=True)  81.8 us
    reduce_scatter x1, waiting for transfers between devices, on_device(): lax.psum_scatter(expert_total[0].astype(jnp.bfloat16), 'dp', scatter_dime...  80.8 us
    all_gather x1, blocking collectives, fetch_attention(): lax.all_gather(attn_local[2], ('dp', 'expert'), axis=0, tiled=True)  47.4 us
    all_to_all x2, waiting for transfers between devices, layer_backward(): lax.all_to_all(grad_received, 'expert', split_axis=0, concat_axis=0, tile...  28.8 us
    dot_general x2, matrix products, layer_backward(): jnp.einsum('rf,rd->fd', activation, grad_rows, preferred_element_type=jnp...  23.6 us
  transfers between devices with their start and end apart: 17, of which 11 were waited for; matrix products, arithmetic and copies ran while one was open for 23% of the time, Pallas kernels for 0%

profile of v1, /device:TPU:0, one launch (start us, length us, event | category | flops | bytes accessed | tf_op | source)
XLA Modules:
  0.0 1022.3 jit_solution(9056450220116369389)
XLA Ops:
  11.0 7.3 all-to-all-start
  20.4 87.6 %all-reduce.5 = (bf16[1024]{0:T(1024)(128)(2,1)S(1)}, bf16[1024]{0:T(1024)(128)(2,1)S(1)}) all-reduce(bf16[1024]{0:T(1024)(128)(2,1)S(1)} %dynamic-update-slice, bf16[1024]{0:T(1024)(128)(2,1)S(1)} %dynamic-update-slice.1), channel_id=1, replica_groups=mesh['dp'=4,'expert'=8] {'dp','expert'}, use_global_device_ids=true, to_apply=%add | all-reduce | flops 2048 | bytes 8192
  154.4 15.8 %all-to-all-done.3 = bf16[8,36,1024]{2,1,0:T(8,128)(2,1)S(1)} async-done(((bf16[8,36,1024]{2,1,0:T(8,128)(2,1)}), bf16[8,36,1024]{2,1,0:T(8,128)(2,1)S(1)}, u32[]{:S(2)}, u32[]{:S(2)}) %all-to-all-start.3) | async-done | bytes 589856 | tf_op jit(solution)/shard_map/all_to_all | solution.py:114
  173.9 13.9 %all-gather.7.cloned.1.call-done = bf16[1,1024,4096]{2,1,0:T(8,128)(2,1)} async-done(((bf16[1,256,4096]{2,1,0:T(8,128)(2,1)}), bf16[1,1024,4096]{2,1,0:T(8,128)(2,1)}) %all-gather.7.cloned.1.call-update) | async-done | bytes 8388624 | tf_op jit(solution)/shard_map/all_gather | solution.py:51
  187.8 7.6 fusion.14
  195.3 81.8 %all-gather.9.cloned.1.call-done = bf16[1,4096,1024]{2,1,0:T(8,128)(2,1)} async-done(((bf16[1,1024,1024]{2,1,0:T(8,128)(2,1)}), bf16[1,4096,1024]{2,1,0:T(8,128)(2,1)}) %all-gather.9.cloned.1.call-update) | async-done | bytes 8388624 | tf_op jit(solution)/shard_map/all_gather | solution.py:52
  277.1 7.8 fusion.49
  312.3 47.4 %all-gather = bf16[32,32,8]{1,2,0:T(8,128)(2,1)S(1)} all-gather(bf16[1,32,8]{1,2,0:T(8,128)(2,1)S(1)} %bitcast.297), channel_id=1, replica_groups=mesh['dp'=4,'expert'=8] {'dp','expert'}, dimensions={0}, use_global_device_ids=true | all-gather | bytes 16896 | tf_op jit(solution)/shard_map/all_gather | solution.py:43
  375.4 15.3 %all-to-all-done.5 = bf16[8,36,1024]{2,1,0:T(8,128)(2,1)S(1)} async-done(((bf16[8,36,1024]{2,1,0:T(8,128)(2,1)}), bf16[8,36,1024]{2,1,0:T(8,128)(2,1)S(1)}, u32[]{:S(2)}, u32[]{:S(2)}) %all-to-all-start.5) | async-done | bytes 589856 | tf_op jit(solution)/shard_map/all_to_all | solution.py:181
  395.9 11.2 %fusion.177 = f32[4096,1024]{1,0:T(8,128)} fusion(bf16[288,1024]{1,0:T(8,128)(2,1)S(1)} %reshape.417, f32[288,4096]{1,0:T(8,128)} %copy-done.16), kind=kOutput, calls=%fused_computation.253 | convolution fusion | flops 2426535936 | bytes 22085632 | tf_op jit(solution)/shard_map/rf,rd->fd/dot_general | solution.py:185
  412.8 12.4 %fusion.1 = bf16[1,4096,1024]{2,1,0:T(8,128)(2,1)} fusion(f32[4096,1024]{1,0:T(8,128)} %fusion.177, bf16[288,1024]{1,0:T(8,128)(2,1)S(1)} %reshape.425, f32[288,4096]{1,0:T(8,128)} %fusion.14), kind=kOutput, calls=%fused_computation.3 | convolution fusion | flops 2434924544 | bytes 30474240 | tf_op jit(solution)/shard_map/rf,rd->fd/dot_general | solution.py:185
  425.5 11.6 %fusion.24 = bf16[288,4096]{1,0:T(8,128)(2,1)S(1)} fusion(f32[288,4096]{1,0:T(8,128)} %copy-done.16, bf16[288,1024]{1,0:T(8,128)(2,1)S(1)} %reshape.417, bf16[1,4096,1024]{2,1,0:T(8,128)(2,1)} %all-gather.9.cloned.1.call-done), kind=kOutput, calls=%fused_computation.31 | convolution fusion | flops 2439512064 | bytes 16056320 | tf_op jit(solution)/shard_map/rd,fd->rf/dot_general | solution.py:184
  437.1 8.2 fusion.186
  445.3 11.6 %fusion.31 = bf16[288,4096]{1,0:T(8,128)(2,1)S(1)} fusion(f32[288,4096]{1,0:T(8,128)} %fusion.14, bf16[288,1024]{1,0:T(8,128)(2,1)S(1)} %reshape.425, bf16[1,4096,1024]{2,1,0:T(8,128)(2,1)} %all-gather.9.cloned.1.call-done), kind=kOutput, calls=%fused_computation.38 | convolution fusion | flops 2439512064 | bytes 16056320 | tf_op jit(solution)/shard_map/rd,fd->rf/dot_general | solution.py:184
  458.3 10.6 %fusion = bf16[1,1024,4096]{2,1,0:T(8,128)(2,1)} fusion(f32[1024,4096]{1,0:T(8,128)} %fusion.186, bf16[288,1024]{1,0:T(8,128)(2,1)S(1)} %copy-done.46, bf16[288,4096]{1,0:T(8,128)(2,1)S(1)} %fusion.31), kind=kOutput, calls=%fused_computation.2 | convolution fusion | flops 2424307712 | bytes 28114944 | tf_op jit(solution)/shard_map/rd,rf->df/dot_general | solution.py:188
  481.1 6.7 fusion.43
  488.8 11.1 %all-to-all-done.6 = bf16[8,36,1024]{2,1,0:T(8,128)(2,1)S(1)} async-done(((bf16[8,36,1024]{2,1,0:T(8,128)(2,1)}), bf16[8,36,1024]{2,1,0:T(8,128)(2,1)S(1)}, u32[]{:S(2)}, u32[]{:S(2)}) %all-to-all-start.6) | async-done | bytes 589856 | tf_op jit(solution)/shard_map/all_to_all | solution.py:191
  505.2 17.7 %all-to-all-done.8 = bf16[8,36,1024]{2,1,0:T(8,128)(2,1)} async-done(((bf16[8,36,1024]{2,1,0:T(8,128)(2,1)}), bf16[8,36,1024]{2,1,0:T(8,128)(2,1)}, u32[]{:S(2)}, u32[]{:S(2)}) %all-to-all-start.8) | async-done | bytes 589856 | tf_op jit(solution)/shard_map/all_to_all | solution.py:191
  559.9 6.8 convolution_add_fusion
  573.4 6.8 fusion.84
  580.2 37.8 %all-reduce.4 = (f32[1024]{0:T(1024)S(1)}, f32[1024]{0:T(1024)S(1)}) all-reduce(f32[1024]{0:T(1024)S(1)} %add.172, f32[1024]{0:T(1024)S(1)} %add.173), channel_id=5, replica_groups=mesh['dp'=4,'expert'=8] {'dp','expert'}, use_global_device_ids=true, to_apply=%region_43.44.clone | all-reduce | flops 2048 | bytes 16384
  629.3 80.8 %reduce-scatter.12.cloned.1.call-done = bf16[1,256,4096]{2,1,0:T(8,128)(2,1)} async-done(((bf16[1,1024,4096]{2,1,0:T(8,128)(2,1)}), bf16[1,256,4096]{2,1,0:T(8,128)(2,1)}) %reduce-scatter.12.cloned.1.call-update) | async-done | bytes 2097168 | tf_op jit(solution)/shard_map/reduce_scatter | solution.py:315
  714.2 142.6 %reduce-scatter.10.cloned.1.call-done = f32[32,1024]{1,0:T(8,128)} async-done(((f32[1024,1024]{1,0:T(8,128)}), f32[32,1024]{1,0:T(8,128)}) %reduce-scatter.10.cloned.1.call-update) | async-done | bytes 131088 | tf_op jit(solution)/shard_map/reduce_scatter | solution.py:309
  856.8 158.5 %reduce-scatter.8.cloned.1.call-done = f32[32,3072]{1,0:T(8,128)} async-done(((f32[1024,3072]{1,0:T(8,128)}), f32[32,3072]{1,0:T(8,128)}) %reduce-scatter.8.cloned.1.call-update) | async-done | bytes 393232 | tf_op jit(solution)/shard_map/reduce_scatter | solution.py:308
  (304 shorter events, 187.7 us)
Async XLA Ops:
  7.2 101.3 %all-gather.5.cloned.1.call-start = ((), (), s32[]{:S(2)}) async-start(), calls=%async_computation.14 | async-start | bytes 6488064 | tf_op jit(solution)/shard_map/all_gather | solution.py:41
  7.9 179.8 %all-gather.7.cloned.1.call-start = ((), (), s32[]{:S(2)}) async-start(), calls=%async_computation.15 | async-start | bytes 10485760 | tf_op jit(solution)/shard_map/all_gather | solution.py:51
  8.7 268.4 %all-gather.9.cloned.1.call-start = ((), (), s32[]{:S(2)}) async-start(), calls=%async_computation.16 | async-start | bytes 10485760 | tf_op jit(solution)/shard_map/all_gather | solution.py:52
  9.5 98.7 %copy-start.65 = (s32[2,1,256]{2,1,0:T(1,128)S(1)}, s32[2,1,256]{2,1,0:T(1,128)}, u32[]{:S(2)}) copy-start(s32[2,1,256]{2,1,0:T(1,128)} %param.12) | copy-start | bytes 6148
  11.0 128.4 %all-to-all-start = ((bf16[32,32,1024]{2,1,0:T(8,128)(2,1)}), bf16[32,32,1024]{2,1,0:T(8,128)(2,1)S(1)}, u32[]{:S(2)}, u32[]{:S(2)}) async-start(bf16[32,32,1024]{2,1,0:T(8,128)(2,1)} %stack.14), calls=%async_computation | async-start | bytes 4194304 | tf_op jit(solution)/shard_map/all_to_all | solution.py:16
  19.2 94.8 %copy-start.57 = (f32[256]{0:T(256)}, f32[256]{0:T(256)S(1)}, u32[]{:S(2)}) copy-start(f32[256]{0:T(256)S(1)} %get-tuple-element.104) | copy-start | bytes 3076
  19.2 102.1 %copy-start.55 = (f32[256]{0:T(256)}, f32[256]{0:T(256)S(1)}, u32[]{:S(2)}) copy-start(f32[256]{0:T(256)S(1)} %get-tuple-element.105) | copy-start | bytes 3076
  19.7 101.7 %copy-start.59 = (f32[256]{0:T(256)}, f32[256]{0:T(256)S(1)}, u32[]{:S(2)}) copy-start(f32[256]{0:T(256)S(1)} %add_rsqrt_fusion.3) | copy-start | bytes 3076
  19.7 94.3 %copy-start.61 = (f32[256]{0:T(256)}, f32[256]{0:T(256)S(1)}, u32[]{:S(2)}) copy-start(f32[256]{0:T(256)S(1)} %add_rsqrt_fusion.1) | copy-start | bytes 3076
  108.3 35.5 %copy-start.38 = (pred[256,256]{0,1:T(8,128)(4,1)}, pred[256,256]{0,1:T(8,128)(4,1)S(1)}, u32[]{:S(2)}) copy-start(pred[256,256]{0,1:T(8,128)(4,1)S(1)} %fusion.112) | copy-start | bytes 196612
  148.4 21.8 %all-to-all-start.3 = ((bf16[8,36,1024]{2,1,0:T(8,128)(2,1)}), bf16[8,36,1024]{2,1,0:T(8,128)(2,1)S(1)}, u32[]{:S(2)}, u32[]{:S(2)}) async-start(bf16[8,36,1024]{2,1,0:T(8,128)(2,1)} %reshape.412), calls=%async_computation.3 | async-start | bytes 1310720 | tf_op jit(solution)/shard_map/all_to_all | solution.py:114
  170.2 115.8 %all-to-all-start.1 = ((bf16[8,36,1024]{2,1,0:T(8,128)(2,1)}), bf16[8,36,1024]{2,1,0:T(8,128)(2,1)S(1)}, u32[]{:S(2)}, u32[]{:S(2)}) async-start(bf16[8,36,1024]{2,1,0:T(8,128)(2,1)} %reshape.404), calls=%async_computation.1 | async-start | bytes 1310720 | tf_op jit(solution)/shard_map/all_to_all | solution.py:114
  286.0 22.7 %all-to-all-start.4 = ((bf16[8,36,1024]{2,1,0:T(8,128)(2,1)}), bf16[8,36,1024]{2,1,0:T(8,128)(2,1)S(1)}, u32[]{:S(2)}, u32[]{:S(2)}) async-start(bf16[8,36,1024]{2,1,0:T(8,128)(2,1)} %reshape.414), calls=%async_computation.4 | async-start | bytes 1310720 | tf_op jit(solution)/shard_map/all_to_all | solution.py:121
  308.7 53.9 %all-to-all-start.2 = ((bf16[8,36,1024]{2,1,0:T(8,128)(2,1)}), bf16[8,36,1024]{2,1,0:T(8,128)(2,1)S(1)}, u32[]{:S(2)}, u32[]{:S(2)}) async-start(bf16[8,36,1024]{2,1,0:T(8,128)(2,1)} %reshape.406), calls=%async_computation.2 | async-start | bytes 1310720 | tf_op jit(solution)/shard_map/all_to_all | solution.py:121
  369.1 21.6 %all-to-all-start.5 = ((bf16[8,36,1024]{2,1,0:T(8,128)(2,1)}), bf16[8,36,1024]{2,1,0:T(8,128)(2,1)S(1)}, u32[]{:S(2)}, u32[]{:S(2)}) async-start(bf16[8,36,1024]{2,1,0:T(8,128)(2,1)} %reshape.416), calls=%async_computation.5 | async-start | bytes 1310720 | tf_op jit(solution)/shard_map/all_to_all | solution.py:181
  390.7 22.0 %all-to-all-start.7 = ((bf16[8,36,1024]{2,1,0:T(8,128)(2,1)}), bf16[8,36,1024]{2,1,0:T(8,128)(2,1)S(1)}, u32[]{:S(2)}, u32[]{:S(2)}) async-start(bf16[8,36,1024]{2,1,0:T(8,128)(2,1)} %reshape.424), calls=%async_computation.7 | async-start | bytes 1310720 | tf_op jit(solution)/shard_map/all_to_all | solution.py:181
  394.2 172.5 %reduce-scatter.16.cloned.1.call-start = ((), (), s32[]{:S(2)}) async-start(), calls=%async_computation.21 | async-start | bytes 540672
  395.7 229.5 %reduce-scatter.14.cloned.1.call-start = ((), (), s32[]{:S(2)}) async-start(), calls=%async_computation.20 | async-start | bytes 10485760 | tf_op jit(solution)/shard_map/reduce_scatter | solution.py:318
  425.2 284.9 %reduce-scatter.12.cloned.1.call-start = ((), (), s32[]{:S(2)}) async-start(), calls=%async_computation.19 | async-start | bytes 10485760 | tf_op jit(solution)/shard_map/reduce_scatter | solution.py:315
  477.5 22.3 %all-to-all-start.6 = ((bf16[8,36,1024]{2,1,0:T(8,128)(2,1)}), bf16[8,36,1024]{2,1,0:T(8,128)(2,1)S(1)}, u32[]{:S(2)}, u32[]{:S(2)}) async-start(bf16[8,36,1024]{2,1,0:T(8,128)(2,1)} %reshape.418), calls=%async_computation.6 | async-start | bytes 1310720 | tf_op jit(solution)/shard_map/all_to_all | solution.py:191
  499.9 23.0 %all-to-all-start.8 = ((bf16[8,36,1024]{2,1,0:T(8,128)(2,1)}), bf16[8,36,1024]{2,1,0:T(8,128)(2,1)}, u32[]{:S(2)}, u32[]{:S(2)}) async-start(bf16[8,36,1024]{2,1,0:T(8,128)(2,1)} %reshape.426), calls=%async_computation.8 | async-start | bytes 1310720 | tf_op jit(solution)/shard_map/all_to_all | solution.py:191
  504.1 352.7 %reduce-scatter.10.cloned.1.call-start = ((), (), s32[]{:S(2)}) async-start(), calls=%async_computation.18 | async-start | bytes 4325376 | tf_op jit(solution)/shard_map/reduce_scatter | solution.py:309
  533.9 481.4 %reduce-scatter.8.cloned.1.call-start = ((), (), s32[]{:S(2)}) async-start(), calls=%async_computation.17 | async-start | bytes 12976128 | tf_op jit(solution)/shard_map/reduce_scatter | solution.py:308
  573.4 48.0 %copy-start.13 = (f32[256,1024]{1,0:T(8,128)S(1)}, f32[256,1024]{1,0:T(8,128)}, u32[]{:S(2)}) copy-start(f32[256,1024]{1,0:T(8,128)} %copy-done.12) | copy-start | bytes 3145732
  (62 other events, 334.2 us)
Sparse Core Ops, SparseCore 0:
  11.0 88.5 all-gather.4
  101.4 86.3 all-gather.6
  189.6 87.4 all-gather.8
  397.0 137.2 reduce-scatter.15
  537.1 83.6 reduce-scatter.13
  623.8 86.2 reduce-scatter.11
  713.0 143.7 reduce-scatter.9
  863.4 151.8 reduce-scatter.7
